TPU v7x, 32 devices: a whole 2x2x4 slice. The times are simulated.
32 devices in a mesh: fsdp: 4 (over y, x), ctx: 4 (over z), tp: 2 (over core).
Axes of the slice: x: 2, y: 2, z: 4, core: 2. Of those that a mesh axis runs over, the one named last changes fastest.
Arguments:
- tokens: bfloat16 [8, 2048, 896], P('fsdp', 'ctx'), may hold values from -6 to 6
- cotangent: bfloat16 [8, 2048, 896], P('fsdp', 'ctx'), may hold values from -6 to 6
- segments: int32 [8, 2048], P('fsdp'), may hold values from 0 to 3, as said below
- positions: int32 [8, 2048], P('fsdp', 'ctx'), may hold values from 0 to 2044, as said below
- norm_one: bfloat16 [896], replicated, may hold values from 0.5 to 1.5
- qkv_weight: bfloat16 [896, 2, 576], P(('fsdp', 'ctx'), 'tp'), may hold values from -0.1875 to 0.1875
- qkv_bias: bfloat16 [2, 576], P('tp'), may hold values from -3 to 3
- out_weight: bfloat16 [896, 896], P(('fsdp', 'ctx'), 'tp'), may hold values from -0.75 to 0.75
- norm_two: bfloat16 [896], replicated, may hold values from 0.5 to 1.5
- gate_weight: bfloat16 [896, 4864], P(('fsdp', 'ctx'), 'tp'), may hold values from -0.1875 to 0.1875
- up_weight: bfloat16 [896, 4864], P(('fsdp', 'ctx'), 'tp'), may hold values from -0.1875 to 0.1875
- down_weight: bfloat16 [896, 4864], P(('fsdp', 'ctx'), 'tp'), may hold values from -0.078125 to 0.078125
Outputs:
- block_out: bfloat16 [8, 2048, 896], P('fsdp', ('ctx', 'tp'))
- input_grad: float32 [8, 2048, 896], P('fsdp', 'ctx')
- norm_one_grad: float32 [896], replicated
- qkv_weight_grad: float32 [896, 2, 576], P(('fsdp', 'ctx'), 'tp')
- qkv_bias_grad: float32 [2, 576], P('tp')
- out_weight_grad: float32 [896, 896], P(('fsdp', 'ctx'), 'tp')
- norm_two_grad: float32 [896], replicated
- gate_weight_grad: float32 [896, 4864], P(('fsdp', 'ctx'), 'tp')
- up_weight_grad: float32 [896, 4864], P(('fsdp', 'ctx'), 'tp')
- down_weight_grad: float32 [896, 4864], P(('fsdp', 'ctx'), 'tp')
Inputs may be any that keep to these rules, and one draw needn't show every extreme that they name: `segments`: each sequence holds exactly 4 documents, numbered from 0 in order, each a contiguous run; the first token is document 0. `positions`: each token's offset from the first token of its document; the largest is reached in every draw.
All inputs are finite; a program needn't handle non-finite values.
Results may differ from a plain program's by a relative error of at most 0.02.
Values may be sent and summed in bfloat16 or wider, within the bound.
No kernel may reach another device: no remote copies, remote signals or barrier semaphores. Data moves between devices by JAX's collectives and lax.ppermute only.
A program may use at most 256 MiB of HBM per device.

v0:
```python
import jax
import jax.numpy as jnp
from jax import lax
from jax.sharding import PartitionSpec as P

HD = 64
GROUP = 7
epsilon = 1e-06
rope_base = 1000000.0
masked_value = -1e30
contract_rows = (((0,), (0,)), ((), ()))
contract_last = (((1,), (1,)), ((), ()))


def rotary_tables(positions):
    half_dim = HD // 2
    frequency = rope_base ** (-(jnp.arange(half_dim, dtype=jnp.float32) * 2.0) / HD)
    angles = positions.astype(jnp.float32)[..., None] * frequency
    cosine = jnp.cos(angles)
    sine_table = jnp.sin(angles)
    return (jnp.concatenate([cosine, cosine], -1), jnp.concatenate([sine_table, sine_table], -1))


def rotate(values, cosine, sine_table):
    half_dim = values.shape[-1] // 2
    turned = jnp.concatenate([-values[..., half_dim:], values[..., :half_dim]], -1)
    return values * cosine + turned * sine_table


def masked_scores(query_one, key_one, own_segment, all_segments, first_row):
    raw_scores = jnp.einsum(
        "qhgd,khd->hgqk", query_one, key_one, preferred_element_type=jnp.float32
    ) * HD ** (-0.5)
    query_index = first_row + jnp.arange(own_segment.shape[0], dtype=jnp.int32)
    key_index = jnp.arange(all_segments.shape[0], dtype=jnp.int32)
    allowed = (own_segment[:, None] == all_segments[None, :]) & (
        key_index[None, :] <= query_index[:, None]
    )
    return jnp.where(allowed, raw_scores, masked_value)


def shards(
    tokens,
    cotangent,
    segments,
    positions,
    norm_one,
    qkv_weight,
    qkv_bias,
    out_weight,
    norm_two,
    gate_weight,
    up_weight,
    down_weight,
):
    seq_count, block_len, model_width = tokens.shape
    row_count = seq_count * block_len
    kv_local = qkv_weight.shape[1]
    per_group = qkv_weight.shape[2]
    q_width = out_weight.shape[1]
    first_row = lax.axis_index("ctx") * block_len
    half_len = block_len // lax.axis_size("tp")
    half_start = lax.axis_index("tp") * half_len

    def own_rows(values):
        return lax.dynamic_slice_in_dim(values, half_start, half_len, 1)

    attention_full = (
        lax.all_gather(qkv_weight, ("fsdp", "ctx"), axis=0, tiled=True),
        lax.all_gather(out_weight, ("fsdp", "ctx"), axis=0, tiled=True),
    )
    qkv_full = attention_full[0].reshape(model_width, kv_local * per_group)
    out_full = attention_full[1]
    inputs_block = tokens.astype(jnp.float32)
    inputs = inputs_block.reshape(row_count, model_width)
    gain_one = norm_one.astype(jnp.float32)
    scale_one = lax.rsqrt(jnp.mean(inputs * inputs, -1, keepdims=True) + epsilon)
    unit_one = inputs * scale_one
    normed = (unit_one * gain_one).astype(jnp.bfloat16)
    projected = jnp.dot(normed, qkv_full, preferred_element_type=jnp.float32) + qkv_bias.astype(
        jnp.float32
    )
    grouped = projected.reshape(seq_count, block_len, kv_local, GROUP + 2, HD)
    cosine, sine_table = rotary_tables(positions)
    queries = rotate(
        grouped[:, :, :, :GROUP], cosine[:, :, None, None], sine_table[:, :, None, None]
    ).astype(jnp.bfloat16)
    key_rows = rotate(grouped[:, :, :, GROUP], cosine[:, :, None], sine_table[:, :, None]).astype(
        jnp.bfloat16
    )
    values = grouped[:, :, :, GROUP + 1].astype(jnp.bfloat16)
    kv_pack = jnp.concatenate([key_rows, values], -1)
    kv_all = lax.all_gather(kv_pack, "ctx", axis=1, tiled=True)
    own_segments = lax.dynamic_slice_in_dim(segments, first_row, block_len, 1)

    def attend(pieces):
        query_one, pack_one, own_segment, all_segments = pieces
        masked = masked_scores(query_one, pack_one[..., :HD], own_segment, all_segments, first_row)
        row_max = jnp.max(masked, -1, keepdims=True)
        exponent = jnp.exp(masked - row_max)
        row_total = jnp.sum(exponent, -1, keepdims=True)
        probability = (exponent / row_total).astype(jnp.bfloat16)
        result = jnp.einsum(
            "hgqk,khd->qhgd", probability, pack_one[..., HD:], preferred_element_type=jnp.float32
        )
        return (result, row_max + jnp.log(row_total))

    attended, log_totals = lax.map(attend, (queries, kv_all, own_segments, segments))
    mixed = attended.reshape(row_count, q_width).astype(jnp.bfloat16)
    branch_part = lax.dot_general(
        mixed, out_full, contract_last, preferred_element_type=jnp.float32
    )
    attention_sum = lax.psum_scatter(
        branch_part.reshape(seq_count, block_len, model_width).astype(jnp.bfloat16),
        "tp",
        scatter_dimension=1,
        tiled=True,
    ).astype(jnp.float32)
    middle = own_rows(inputs_block) + attention_sum
    feed_full = (
        lax.all_gather(gate_weight, ("fsdp", "ctx"), axis=0, tiled=True),
        lax.all_gather(up_weight, ("fsdp", "ctx"), axis=0, tiled=True),
        lax.all_gather(down_weight, ("fsdp", "ctx"), axis=0, tiled=True),
    )
    gate_full, up_full, down_full = feed_full
    gain_two = norm_two.astype(jnp.float32)
    scale_two = lax.rsqrt(jnp.mean(middle * middle, -1, keepdims=True) + epsilon)
    unit_two = middle * scale_two
    normed_two_half = (unit_two * gain_two).astype(jnp.bfloat16)
    normed_two = lax.all_gather(normed_two_half, "tp", axis=1, tiled=True).reshape(
        row_count, model_width
    )
    gate_act = jnp.dot(normed_two, gate_full, preferred_element_type=jnp.float32)
    up_act = jnp.dot(normed_two, up_full, preferred_element_type=jnp.float32)
    silu_gate = jax.nn.silu(gate_act)
    hidden = (silu_gate * up_act).astype(jnp.bfloat16)
    feed_part = lax.dot_general(
        hidden, down_full, contract_last, preferred_element_type=jnp.float32
    )
    feed_sum = lax.psum_scatter(
        feed_part.reshape(seq_count, block_len, model_width).astype(jnp.bfloat16),
        "tp",
        scatter_dimension=1,
        tiled=True,
    ).astype(jnp.float32)
    block_out = (middle + feed_sum).astype(jnp.bfloat16)
    attention_back = (
        lax.all_gather(qkv_weight, ("fsdp", "ctx"), axis=0, tiled=True),
        lax.all_gather(out_weight, ("fsdp", "ctx"), axis=0, tiled=True),
    )
    feed_back = (
        lax.all_gather(gate_weight, ("fsdp", "ctx"), axis=0, tiled=True),
        lax.all_gather(up_weight, ("fsdp", "ctx"), axis=0, tiled=True),
        lax.all_gather(down_weight, ("fsdp", "ctx"), axis=0, tiled=True),
    )
    qkv_back = attention_back[0].reshape(model_width, kv_local * per_group)
    out_back = attention_back[1]
    gate_back, up_back, down_back = feed_back
    upstream_low = cotangent.reshape(row_count, model_width)
    upstream_half = own_rows(cotangent).astype(jnp.float32)
    hidden_grad = jnp.dot(upstream_low, down_back, preferred_element_type=jnp.float32)
    down_weight_grad = lax.dot_general(
        upstream_low, hidden, contract_rows, preferred_element_type=jnp.float32
    )
    sigmoid = jax.nn.sigmoid(gate_act)
    gate_grad = (hidden_grad * up_act * (sigmoid * (1.0 + gate_act * (1.0 - sigmoid)))).astype(
        jnp.bfloat16
    )
    up_grad = (hidden_grad * silu_gate).astype(jnp.bfloat16)
    normed_two_part = lax.dot_general(
        gate_grad, gate_back, contract_last, preferred_element_type=jnp.float32
    )
    normed_two_part = normed_two_part + lax.dot_general(
        up_grad, up_back, contract_last, preferred_element_type=jnp.float32
    )
    gate_weight_grad = lax.dot_general(
        normed_two, gate_grad, contract_rows, preferred_element_type=jnp.float32
    )
    up_weight_grad = lax.dot_general(
        normed_two, up_grad, contract_rows, preferred_element_type=jnp.float32
    )
    feed_grads = (
        lax.psum_scatter(gate_weight_grad, ("fsdp", "ctx"), scatter_dimension=0, tiled=True),
        lax.psum_scatter(up_weight_grad, ("fsdp", "ctx"), scatter_dimension=0, tiled=True),
        lax.psum_scatter(down_weight_grad, ("fsdp", "ctx"), scatter_dimension=0, tiled=True),
    )
    normed_two_grad = lax.psum_scatter(
        normed_two_part.reshape(seq_count, block_len, model_width).astype(jnp.bfloat16),
        "tp",
        scatter_dimension=1,
        tiled=True,
    ).astype(jnp.float32)
    gain_two_grad = jnp.sum(normed_two_grad * unit_two, (0, 1))
    scaled_two = normed_two_grad * gain_two
    middle_grad = upstream_half + scale_two * (
        scaled_two - unit_two * jnp.mean(scaled_two * unit_two, -1, keepdims=True)
    )
    branch_half = middle_grad.astype(jnp.bfloat16)
    branch_low = lax.all_gather(branch_half, "tp", axis=1, tiled=True).reshape(
        row_count, model_width
    )
    mixed_grad = jnp.dot(branch_low, out_back, preferred_element_type=jnp.float32).astype(
        jnp.bfloat16
    )
    out_weight_grad = lax.dot_general(
        branch_low, mixed, contract_rows, preferred_element_type=jnp.float32
    )
    mixed_heads = mixed_grad.reshape(seq_count, block_len, kv_local, GROUP, HD)

    def attend_back(pieces):
        query_one, pack_one, own_segment, all_segments, log_one, grad_one = pieces
        key_one = pack_one[..., :HD]
        value_one = pack_one[..., HD:]
        masked = masked_scores(query_one, key_one, own_segment, all_segments, first_row)
        probability = jnp.exp(masked - log_one)
        value_grad = jnp.einsum(
            "hgqk,qhgd->khd",
            probability.astype(jnp.bfloat16),
            grad_one,
            preferred_element_type=jnp.float32,
        )
        prob_grad = jnp.einsum(
            "qhgd,khd->hgqk", grad_one, value_one, preferred_element_type=jnp.float32
        )
        centre = jnp.sum(probability * prob_grad, -1, keepdims=True)
        score_grad = (probability * (prob_grad - centre)).astype(jnp.bfloat16)
        query_grad = jnp.einsum(
            "hgqk,khd->qhgd", score_grad, key_one, preferred_element_type=jnp.float32
        ) * HD ** (-0.5)
        key_grad = jnp.einsum(
            "hgqk,qhgd->khd", score_grad, query_one, preferred_element_type=jnp.float32
        ) * HD ** (-0.5)
        return (query_grad, jnp.concatenate([key_grad, value_grad], -1))

    query_grads, pack_grads = lax.map(
        attend_back, (queries, kv_all, own_segments, segments, log_totals, mixed_heads)
    )
    pack_sum = lax.psum_scatter(
        pack_grads.astype(jnp.bfloat16), "ctx", scatter_dimension=1, tiled=True
    ).astype(jnp.float32)
    query_turned = rotate(query_grads, cosine[:, :, None, None], -sine_table[:, :, None, None])
    key_turned = rotate(pack_sum[..., :HD], cosine[:, :, None], -sine_table[:, :, None])
    grouped_grad = jnp.concatenate(
        [query_turned, key_turned[:, :, :, None], pack_sum[:, :, :, None, HD:]], 3
    )
    projected_grad = grouped_grad.reshape(row_count, kv_local * per_group).astype(jnp.bfloat16)
    bias_grad = jnp.sum(projected_grad.astype(jnp.float32), 0).reshape(kv_local, per_group)
    normed_one_part = lax.dot_general(
        projected_grad, qkv_back, contract_last, preferred_element_type=jnp.float32
    )
    qkv_weight_grad = lax.dot_general(
        normed, projected_grad, contract_rows, preferred_element_type=jnp.float32
    )
    qkv_shaped = qkv_weight_grad.reshape(model_width, kv_local, per_group)
    attention_grads = (
        lax.psum_scatter(qkv_shaped, ("fsdp", "ctx"), scatter_dimension=0, tiled=True),
        lax.psum_scatter(out_weight_grad, ("fsdp", "ctx"), scatter_dimension=0, tiled=True),
    )
    normed_one_grad = lax.psum_scatter(
        normed_one_part.reshape(seq_count, block_len, model_width).astype(jnp.bfloat16),
        "tp",
        scatter_dimension=1,
        tiled=True,
    ).astype(jnp.float32)
    unit_one_half = own_rows(unit_one.reshape(seq_count, block_len, model_width))
    scale_one_half = own_rows(scale_one.reshape(seq_count, block_len, 1))
    gain_one_grad = jnp.sum(normed_one_grad * unit_one_half, (0, 1))
    scaled_one = normed_one_grad * gain_one
    input_half = middle_grad + scale_one_half * (
        scaled_one - unit_one_half * jnp.mean(scaled_one * unit_one_half, -1, keepdims=True)
    )
    gain_pair = jnp.stack([gain_one_grad, gain_two_grad])[None]
    gathered = (
        lax.all_gather(input_half.astype(jnp.bfloat16), "tp", axis=1, tiled=True).astype(
            input_half.dtype
        ),
        lax.all_gather(gain_pair.astype(jnp.bfloat16), "tp", axis=0, tiled=True).astype(
            gain_pair.dtype
        ),
    )
    input_grad = gathered[0]
    gain_total = jnp.sum(gathered[1], 0)
    small_grads = lax.psum((gain_total, bias_grad), ("fsdp", "ctx"))
    return (
        block_out,
        input_grad,
        small_grads[0][0],
        attention_grads[0],
        small_grads[1],
        attention_grads[1],
        small_grads[0][1],
        feed_grads[0],
        feed_grads[1],
        feed_grads[2],
    )


def solution(mesh):
    return jax.shard_map(
        shards,
        mesh=mesh,
        in_specs=(
            P("fsdp", "ctx", None),
            P("fsdp", "ctx", None),
            P("fsdp", None),
            P("fsdp", "ctx"),
            P(),
            P(("fsdp", "ctx"), "tp", None),
            P("tp", None),
            P(("fsdp", "ctx"), "tp"),
            P(),
            P(("fsdp", "ctx"), "tp"),
            P(("fsdp", "ctx"), "tp"),
            P(("fsdp", "ctx"), "tp"),
        ),
        out_specs=(
            P("fsdp", ("ctx", "tp"), None),
            P("fsdp", "ctx", None),
            P(),
            P(("fsdp", "ctx"), "tp", None),
            P("tp", None),
            P(("fsdp", "ctx"), "tp"),
            P(),
            P(("fsdp", "ctx"), "tp"),
            P(("fsdp", "ctx"), "tp"),
            P(("fsdp", "ctx"), "tp"),
        ),
        check_vma=False,
    )
```

profile of v0, /device:TPU:0, one launch (start us, length us, event | category | flops | bytes accessed | tf_op | source)
XLA Modules:
  0.0 1616.5 jit_solution(670635166496155173)
XLA Ops:
  10.7 54.7 %all_gather.35 = bf16[896,1,576]{2,0,1:T(8,128)(2,1)S(1)} all-gather(bf16[56,1,576]{2,0,1:T(8,128)(2,1)} %param.21), channel_id=1, replica_groups=mesh['fsdp'=4,'ctx'=4,'tp'=2] {'fsdp','ctx'}, dimensions={0}, use_global_device_ids=true | all-gather | bytes 1096704 | tf_op jit(solution)/shard_map/all_gather | solution.py:69
  84.3 54.6 %all_gather.37 = bf16[896,448]{1,0:T(8,128)(2,1)} all-gather(bf16[56,448]{1,0:T(8,128)(2,1)S(1)} %copy-done.37), channel_id=1, replica_groups=mesh['fsdp'=4,'ctx'=4,'tp'=2] {'fsdp','ctx'}, dimensions={0}, use_global_device_ids=true | all-gather | bytes 852992 | tf_op jit(solution)/shard_map/all_gather | solution.py:70
  138.9 81.7 %while.26 = (s32[]{:T(128)}, bf16[2,512,1,7,64]{1,4,3,2,0:T(8,128)(2,1)}, f32[2,1,7,512,1]{3,2,4,1,0:T(8,128)S(1)}, bf16[2,2048,1,128]{1,3,2,0:T(8,128)(2,1)}, s...) while((s32[]{:T(128)}, ...), condition=%wide.region_4.5_spmd.clone, body=%wide.region_1.4_spmd.sunk.clone | while | flops 1970271232 | bytes 102723752 | solution.py:108
  141.0 11.9 fusion.158
  152.9 12.8 fusion.159
  165.8 13.0 fusion.160
  181.8 11.9 fusion.158
  193.8 12.8 fusion.159
  206.7 13.0 fusion.160
  246.5 81.2 %all-gather.14.cloned.1.call-done = bf16[896,2432]{1,0:T(8,128)(2,1)} async-done(((bf16[56,2432]{1,0:T(8,128)(2,1)}), bf16[896,2432]{1,0:T(8,128)(2,1)}) %all-gather.14.cloned.1.call-update) | async-done | bytes 4358160 | tf_op jit(solution)/shard_map/all_gather | solution.py:122
  338.2 68.3 %all-gather.12.cloned.1.call-done = bf16[896,2432]{1,0:T(8,128)(2,1)} async-done(((bf16[56,2432]{1,0:T(8,128)(2,1)}), bf16[896,2432]{1,0:T(8,128)(2,1)}) %all-gather.12.cloned.1.call-update) | async-done | bytes 4358160 | tf_op jit(solution)/shard_map/all_gather | solution.py:121
  416.9 68.2 %all-gather.16.cloned.1.call-done = bf16[896,2432]{1,0:T(8,128)(2,1)} async-done(((bf16[56,2432]{1,0:T(8,128)(2,1)}), bf16[896,2432]{1,0:T(8,128)(2,1)}) %all-gather.16.cloned.1.call-update) | async-done | bytes 4358160 | tf_op jit(solution)/shard_map/all_gather | solution.py:123
  485.1 17.8 %multiply_convert_fusion = (bf16[1024,2432]{1,0:T(8,128)(2,1)}, bf16[1024,2432]{1,0:T(8,128)(2,1)}, bf16[1024,2432]{1,0:T(8,128)(2,1)}) fusion(f32[1024,2432]{1,0:T(8,128)} %fusion.83, f32[1024,2432]{1,0:T(8,128)} %fusion.84, bf16[1024,896]{1,0:T(8,128)(2,1)} %bitcast.347, bf16[896,2432]{1,0:T(8,128)(2,1)} %all-gather.16.cloned.1.call-done), kind=kOutput, calls=%fused_computation.67 | convolution fusion | flops 4500094976 | bytes 41058304 | tf_op jit(solution)/shard_map/dot_general | solution.py:161
  531.9 11.4 all-gather.18.cloned.1.call-done
  549.1 188.6 %while.27 = (s32[]{:T(128)}, f32[2,512,1,7,64]{1,4,3,2,0:T(8,128)}, bf16[2,2048,1,128]{1,3,2,0:T(8,128)(2,1)}, bf16[2,2048,1,128]{1,3,2,0:T(8,128)(2,1)}, s32[2,...) while((s32[]{:T(128)}, f32[2,512,1,7,64]{1,4,3,2,0:T(8,128)}, ...), condition=%wide.region_12.13_spmd.clone, body=%wide.region_10.12_spmd.sunk.clone | while | flops 4768363520 | bytes 251635968 | solution.py:235
  551.7 11.8 fusion.167
  563.5 21.3 %fusion.169 = (f32[7,512]{1,0:T(8,128)S(1)}, f32[1,7,512,2048]{2,3,1,0:T(8,128)}) fusion(f32[2048,512,7]{1,0,2:T(8,128)} %fusion.167, f32[7,512]{1,0:T(8,128)S(1)} %dynamic-slice_bitcast_fusion.11, bf16[2,512,1,7,64]{1,4,3,2,0:T(8,128)(2,1)S(1)} %get-tuple-element.480, s32[]{:T(128)S(6)} %copy.121, ...), kind=kOutput, calls=%fused_computation.29.clone.1.clone | convolution fusion | flops 976220672 | bytes 60520452 | tf_op jit(solution)/shard_map/while/body/eval_jaxpr/qhgd,khd->hgqk/dot_general | solution.py:31
  584.8 25.0 %fusion.170 = bf16[7,512,2048]{1,2,0:T(8,128)(2,1)} fusion(f32[1,7,512,2048]{2,3,1,0:T(8,128)} %get-tuple-element.416, f32[2048,512,7]{1,0,2:T(8,128)} %fusion.167, f32[7,512]{1,0:T(8,128)S(1)} %get-tuple-element.417), kind=kLoop, calls=%fused_computation.32.clone.1.clone | loop fusion | flops 22020096 | bytes 73414656 | tf_op jit(solution)/shard_map/reshape.37
  609.7 13.9 fusion.172
  645.7 11.8 fusion.167
  657.5 21.3 %fusion.169 = (f32[7,512]{1,0:T(8,128)S(1)}, f32[1,7,512,2048]{2,3,1,0:T(8,128)}) fusion(f32[2048,512,7]{1,0,2:T(8,128)} %fusion.167, f32[7,512]{1,0:T(8,128)S(1)} %dynamic-slice_bitcast_fusion.11, bf16[2,512,1,7,64]{1,4,3,2,0:T(8,128)(2,1)S(1)} %get-tuple-element.480, s32[]{:T(128)S(6)} %copy.121, ...), kind=kOutput, calls=%fused_computation.29.clone.1.clone | convolution fusion | flops 976220672 | bytes 60520452 | tf_op jit(solution)/shard_map/while/body/eval_jaxpr/qhgd,khd->hgqk/dot_general | solution.py:31
  678.8 25.0 %fusion.170 = bf16[7,512,2048]{1,2,0:T(8,128)(2,1)} fusion(f32[1,7,512,2048]{2,3,1,0:T(8,128)} %get-tuple-element.416, f32[2048,512,7]{1,0,2:T(8,128)} %fusion.167, f32[7,512]{1,0:T(8,128)S(1)} %get-tuple-element.417), kind=kLoop, calls=%fused_computation.32.clone.1.clone | loop fusion | flops 22020096 | bytes 73414656 | tf_op jit(solution)/shard_map/reshape.37
  703.8 13.9 fusion.172
  740.5 25.8 %reduce-scatter.22.cloned.1.call-done = bf16[2,512,1,128]{1,3,2,0:T(8,128)(2,1)} async-done(((bf16[2,2048,1,128]{1,3,2,0:T(8,128)(2,1)}), bf16[2,512,1,128]{1,3,2,0:T(8,128)(2,1)}) %reduce-scatter.22.cloned.1.call-update) | async-done | bytes 262160 | tf_op jit(solution)/shard_map/reduce_scatter | solution.py:238
  798.4 11.9 convolution_bitcast_fusion.1
  822.3 11.4 fusion.88
  833.8 10.7 fusion.87
  848.3 48.3 %all-reduce.4 = (f32[2,896]{1,0:T(2,128)S(1)}, f32[1,576]{1,0:T(1,128)}) all-reduce(f32[2,896]{1,0:T(2,128)S(1)} %convert_reduce_fusion.1, f32[1,576]{1,0:T(1,128)S(1)} %reshape.576), channel_id=1, replica_groups=mesh['fsdp'=4,'ctx'=4,'tp'=2] {'fsdp','ctx'}, use_global_device_ids=true, to_apply=%region_19.20 | all-reduce | flops 2368 | bytes 18944 | tf_op jit(solution)/shard_map/psum | solution.py:283
  900.8 243.7 %all-reduce.8.cloned.1.call-done = (f32[896,1,576]{2,1,0:T(1,128)}, f32[896,2432]{0,1:T(8,128)}) async-done(((f32[896,1,576]{2,1,0:T(1,128)}, f32[896,2432]{0,1:T(8,128)}), (f32[896,1,576]{2,1,0:T(1,128)}, f32[896,2432]{0,1:T(8,128)})) %all-reduce.8.cloned.1.call-update) | async-done | bytes 10780688
  1149.4 80.0 %reduce-scatter.26.cloned.1.call-done = f32[56,448]{1,0:T(8,128)} async-done(((f32[896,448]{1,0:T(8,128)}), f32[56,448]{1,0:T(8,128)}) %reduce-scatter.26.cloned.1.call-update) | async-done | bytes 100368 | tf_op jit(solution)/shard_map/reduce_scatter | solution.py:257
  1229.4 189.6 %reduce-scatter.30.cloned.1.call-done = f32[56,2432]{1,0:T(8,128)} async-done(((f32[896,2432]{1,0:T(8,128)}), f32[56,2432]{1,0:T(8,128)}) %reduce-scatter.30.cloned.1.call-update) | async-done | bytes 544784
  1419.0 190.7 %reduce-scatter.28.cloned.1.call-done = f32[56,2432]{1,0:T(8,128)} async-done(((f32[896,2432]{1,0:T(8,128)}), f32[56,2432]{1,0:T(8,128)}) %reduce-scatter.28.cloned.1.call-update) | async-done | bytes 544784
  (264 shorter events, 212.2 us)
Async XLA Ops:
  7.2 58.2 %copy-start.3 = (bf16[2,512,896]{2,1,0:T(8,128)(2,1)S(1)}, bf16[2,512,896]{2,1,0:T(8,128)(2,1)}, u32[]{:S(2)}) copy-start(bf16[2,512,896]{2,1,0:T(8,128)(2,1)} %param.16) | copy-start | bytes 5505028
  7.2 131.7 %all-gather.8.cloned.1.call-start = ((), (), s32[]{:S(2)}) async-start(), calls=%async_computation.8 | async-start | bytes 1310720 | tf_op jit(solution)/shard_map/all_gather | solution.py:93
  8.1 59.7 %copy-start.35 = (f32[896]{0:T(1024)}, f32[896]{0:T(1024)S(1)}, u32[]{:S(2)}) copy-start(f32[896]{0:T(1024)S(1)} %convert_element_type.184) | copy-start | bytes 10756
  10.7 57.0 %copy-start.40 = (f32[2,512]{1,0:T(2,128)}, f32[2,512]{1,0:T(2,128)S(1)}, u32[]{:S(2)}) copy-start(f32[2,512]{1,0:T(2,128)S(1)} %add_rsqrt_fusion) | copy-start | bytes 12292
  76.9 154.7 %reduce-scatter.16.cloned.1.call-start = ((), (), s32[]{:S(2)}) async-start(), calls=%async_computation.9 | async-start | bytes 2752512 | tf_op jit(solution)/shard_map/reduce_scatter | solution.py:113
  83.5 55.4 %copy-start.31 = (f32[2,1,7,512,1]{3,2,4,1,0:T(8,128)S(1)}, f32[2,1,7,512,1]{3,2,4,1,0:T(8,128)}, u32[]{:S(2)}) copy-start(f32[2,1,7,512,1]{3,2,4,1,0:T(8,128)} %custom-call) | copy-start | bytes 86020
  83.5 55.4 %copy-start.32 = (s32[2,512]{1,0:T(2,128)S(1)}, s32[2,512]{1,0:T(2,128)}, u32[]{:S(2)}) copy-start(s32[2,512]{1,0:T(2,128)} %constant_dynamic-slice_fusion.5) | copy-start | bytes 12292
  152.9 12.9 copy-start.13
  193.8 12.9 copy-start.13
  224.8 21.7 %all-gather.10.cloned.1.call-start = ((), (), s32[]{:S(2)}) async-start(), calls=%async_computation.10 | async-start | bytes 2752512 | tf_op jit(solution)/shard_map/all_gather | solution.py:130
  226.9 303.3 %copy-start.33 = (f32[896]{0:T(1024)}, f32[896]{0:T(1024)S(1)}, u32[]{:S(2)}) copy-start(f32[896]{0:T(1024)S(1)} %convert_element_type.195) | copy-start | bytes 10756
  233.7 296.5 %copy-start = (f32[2,256,896]{2,1,0:T(8,128)}, f32[2,256,896]{2,1,0:T(8,128)S(1)}, u32[]{:S(2)}) copy-start(f32[2,256,896]{2,1,0:T(8,128)S(1)} %get-tuple-element.243) | copy-start | bytes 5505028
  233.7 296.5 %copy-start.38 = (f32[2,256]{1,0:T(2,128)}, f32[2,256]{1,0:T(2,128)S(1)}, u32[]{:S(2)}) copy-start(f32[2,256]{1,0:T(2,128)S(1)} %add_rsqrt_fusion.1) | copy-start | bytes 6148
  235.1 92.7 %all-gather.14.cloned.1.call-start = ((), (), s32[]{:S(2)}) async-start(), calls=%async_computation.12 | async-start | bytes 4630528 | tf_op jit(solution)/shard_map/all_gather | solution.py:122
  235.6 170.8 %all-gather.12.cloned.1.call-start = ((), (), s32[]{:S(2)}) async-start(), calls=%async_computation.11 | async-start | bytes 4630528 | tf_op jit(solution)/shard_map/all_gather | solution.py:121
  236.2 248.9 %all-gather.16.cloned.1.call-start = ((), (), s32[]{:S(2)}) async-start(), calls=%async_computation.13 | async-start | bytes 4630528 | tf_op jit(solution)/shard_map/all_gather | solution.py:123
  236.8 290.8 %reduce-scatter.20.cloned.1.call-start = ((), (), s32[]{:S(2)}) async-start(), calls=%async_computation.15 | async-start | bytes 2752512 | tf_op jit(solution)/shard_map/reduce_scatter | solution.py:187
  485.1 17.8 %copy-start.47 = (bf16[896,2432]{1,0:T(8,128)(2,1)S(1)}, bf16[896,2432]{1,0:T(8,128)(2,1)}, u32[]{:S(2)}) copy-start(bf16[896,2432]{1,0:T(8,128)(2,1)} %all-gather.12.cloned.1.call-done) | copy-start | bytes 13074436
  519.5 23.8 %all-gather.18.cloned.1.call-start = ((), (), s32[]{:S(2)}) async-start(), calls=%async_computation.16 | async-start | bytes 2752512 | tf_op jit(solution)/shard_map/all_gather | solution.py:199
  531.8 234.5 %reduce-scatter.22.cloned.1.call-start = ((), (), s32[]{:S(2)}) async-start(), calls=%async_computation.17 | async-start | bytes 1310720 | tf_op jit(solution)/shard_map/reduce_scatter | solution.py:238
  737.8 45.6 %reduce-scatter.24.cloned.1.call-start = ((), (), s32[]{:S(2)}) async-start(), calls=%async_computation.18 | async-start | bytes 2752512 | tf_op jit(solution)/shard_map/reduce_scatter | solution.py:259
  739.9 28.3 %copy-start.22 = (f32[2,512,32]{1,2,0:T(8,128)S(1)}, f32[2,512,32]{1,2,0:T(8,128)}, u32[]{:S(2)}) copy-start(f32[2,512,32]{1,2,0:T(8,128)} %copy-done.21) | copy-start | bytes 393220
  739.9 28.3 %copy-start.24 = (f32[2,512,1,32]{1,3,0,2:T(8,128)S(1)}, f32[2,512,1,32]{1,3,0,2:T(8,128)}, u32[]{:S(2)}) copy-start(f32[2,512,1,32]{1,3,0,2:T(8,128)} %copy-done.23) | copy-start | bytes 393220
  740.5 30.0 %copy-start.26 = (bf16[896,1,576]{2,0,1:T(8,128)(2,1)S(1)}, bf16[896,1,576]{2,0,1:T(8,128)(2,1)}, u32[]{:S(2)}) copy-start(bf16[896,1,576]{2,0,1:T(8,128)(2,1)} %copy-done.25) | copy-start | bytes 3096580
  773.6 21.0 %reduce-scatter.18.cloned.1.call-start = ((), (), s32[]{:S(2)}) async-start(), calls=%async_computation.14 | async-start | bytes 2752512 | tf_op jit(solution)/shard_map/reduce_scatter | solution.py:140
  783.3 11.3 copy-start.34
  783.4 113.9 %all-gather.20.cloned.1.call-start = ((), (), s32[]{:S(2)}) async-start(), calls=%async_computation.19 | async-start | bytes 2752512 | tf_op jit(solution)/shard_map/all_gather | solution.py:274
  798.4 11.9 copy-start.11
  798.4 346.2 %all-reduce.8.cloned.1.call-start = ((), (), s32[]{:S(2)}) async-start(), calls=%async_computation.23 | async-start | bytes 22020096
  816.9 412.5 %reduce-scatter.26.cloned.1.call-start = ((), (), s32[]{:S(2)}) async-start(), calls=%async_computation.20 | async-start | bytes 1949696 | tf_op jit(solution)/shard_map/reduce_scatter | solution.py:257
  822.0 597.0 %reduce-scatter.30.cloned.1.call-start = ((), (), s32[]{:S(2)}) async-start(), calls=%async_computation.22 | async-start | bytes 9261056
  833.7 776.0 %reduce-scatter.28.cloned.1.call-start = ((), (), s32[]{:S(2)}) async-start(), calls=%async_computation.21 | async-start | bytes 9261056
  (43 other events, 171.4 us)
Sparse Core Ops, SparseCore 0:
  77.0 31.9 all-gather.7
  224.9 6.6 reduce-scatter.15
  235.2 11.3 all-gather.9
  249.4 78.2 all-gather.13
  330.7 75.7 all-gather.11
  409.3 75.7 all-gather.15
  519.6 7.9 reduce-scatter.19
  531.9 11.3 all-gather.17
  738.0 28.3 reduce-scatter.21
  773.7 7.9 reduce-scatter.23
  784.0 10.5 reduce-scatter.17
  798.5 11.3 all-gather.19
  817.4 327.0 all-reduce.7
  1147.3 81.9 reduce-scatter.25
  1232.1 186.8 reduce-scatter.29
  1421.8 187.9 reduce-scatter.27
where the time goes:
time: 1620 us
  waiting for transfers between devices  992 us (61%)
  matrix products  295 us (18%)
  blocking collectives  159 us (10%)
  other arithmetic  113 us (7%)
  local copies, waits for them, and re-layouts  40.6 us (3%)
    unnamed x19, waiting for transfers between devices  626 us
    all_gather x1, waiting for transfers between devices, shards(): lax.all_gather(up_weight, ('fsdp', 'ctx'), axis=0, tiled=True)  81.2 us
    reduce_scatter x1, waiting for transfers between devices, shards(): lax.psum_scatter(out_weight_grad, ('fsdp', 'ctx'), scatter_dimension=0, t...  80 us
    all_gather x1, waiting for transfers between devices, shards(): lax.all_gather(gate_weight, ('fsdp', 'ctx'), axis=0, tiled=True)  68.3 us
    all_gather x1, waiting for transfers between devices, shards(): lax.all_gather(down_weight, ('fsdp', 'ctx'), axis=0, tiled=True)  68.2 us
    dot_general x4, matrix products, masked_scores(): jnp.einsum('qhgd,khd->hgqk', query_one, key_one, preferred_element_type=j...  66.4 us
    all_gather x1, blocking collectives, shards(): lax.all_gather(qkv_weight, ('fsdp', 'ctx'), axis=0, tiled=True)  54.7 us
    all_gather x1, blocking collectives, shards(): lax.all_gather(out_weight, ('fsdp', 'ctx'), axis=0, tiled=True)  54.6 us
  transfers between devices with their start and end apart: 16, of which 13 were waited for; matrix products, arithmetic and copies ran while one was open for 6% of the time, Pallas kernels for 0%

commit v1 on v0

--- a/solution.py
+++ b/solution.py
@@ -10,6 +10,34 @@
 masked_value = -1e30
 contract_rows = (((0,), (0,)), ((), ()))
 contract_last = (((1,), (1,)), ((), ()))
+
+
+def mix_the_sections(here_x, comm_axis):
+    later = lax.psum(1, axis_name=comm_axis)
+    far_arr = lax.axis_index(comm_axis)
+    everything, val2, r2 = (later, far_arr, here_x.shape[0])
+    latest = jnp.zeros(
+        [h * everything if dev_i == 0 else h for dev_i, h in enumerate(here_x.shape)], here_x.dtype
+    )
+    local_now = piece_out = here_x
+    vec_out = lax.dynamic_update_slice_in_dim(latest, here_x, val2 * r2, axis=0)
+    for ix in range(1, everything // 2 + 1):
+        heard = range(everything)
+        m_next = map(lambda dev_i: (dev_i, (dev_i + 1) % everything), heard)
+        extra = list(m_next)
+        local_now = lax.ppermute(local_now, axis_name=comm_axis, perm=extra)
+        vec_out = lax.dynamic_update_slice_in_dim(
+            vec_out, local_now, (val2 - ix) % everything * r2, axis=0
+        )
+        if 2 * ix < everything:
+            f_now = range(everything)
+            part_now = map(lambda dev_i: (dev_i, (dev_i - 1) % everything), f_now)
+            local_part = list(part_now)
+            piece_out = lax.ppermute(piece_out, comm_axis, local_part)
+            vec_out = lax.dynamic_update_slice_in_dim(
+                vec_out, piece_out, (val2 + ix) % everything * r2, axis=0
+            )
+    return vec_out
 
 
 def rotary_tables(positions):
@@ -67,7 +95,7 @@
 
     attention_full = (
         lax.all_gather(qkv_weight, ("fsdp", "ctx"), axis=0, tiled=True),
-        lax.all_gather(out_weight, ("fsdp", "ctx"), axis=0, tiled=True),
+        mix_the_sections(out_weight, ("fsdp", "ctx")),
     )
     qkv_full = attention_full[0].reshape(model_width, kv_local * per_group)
     out_full = attention_full[1]

time: 1620 us -> 1670 us (1.031)
  starting transfers between devices: 1.04 us -> 42.9 us
    ppermute x0 -> x15, starting transfers between devices: none -> 42.1 us  [the longest x7 41.8 us: mix_the_sections(): piece_out = lax.ppermute(piece_out, comm_axis, local_part)]
  transfers between devices with their start and end apart: 16 -> 31, of which waited for: 13 -> 24; matrix products, arithmetic and copies ran while one was open for 6% -> 7% of each run, Pallas kernels for 0% -> 0%
where the time goes in v1:
time: 1670 us
  waiting for transfers between devices  993 us (59%)
  matrix products  295 us (18%)
  blocking collectives  155 us (9%)
  other arithmetic  112 us (7%)
  local copies, waits for them, and re-layouts  50.1 us (3%)
  starting transfers between devices  42.9 us (3%)
    unnamed x19, waiting for transfers between devices  626 us
    all_gather x1, waiting for transfers between devices, shards(): lax.all_gather(gate_weight, ('fsdp', 'ctx'), axis=0, tiled=True)  81.2 us
    reduce_scatter x1, waiting for transfers between devices, shards(): lax.psum_scatter(out_weight_grad, ('fsdp', 'ctx'), scatter_dimension=0, t...  79.3 us
    all_gather x1, waiting for transfers between devices, shards(): lax.all_gather(down_weight, ('fsdp', 'ctx'), axis=0, tiled=True)  68.3 us
    all_gather x1, waiting for transfers between devices, shards(): lax.all_gather(up_weight, ('fsdp', 'ctx'), axis=0, tiled=True)  68 us
    dot_general x4, matrix products, masked_scores(): jnp.einsum('qhgd,khd->hgqk', query_one, key_one, preferred_element_type=j...  66.5 us
    all_gather x1, blocking collectives, shards(): lax.all_gather(qkv_weight, ('fsdp', 'ctx'), axis=0, tiled=True)  54.7 us
    another operation x4, other arithmetic  50.5 us
  transfers between devices with their start and end apart: 31, of which 24 were waited for; matrix products, arithmetic and copies ran while one was open for 7% of the time, Pallas kernels for 0%

profile of v1, /device:TPU:0, one launch (start us, length us, event | category | flops | bytes accessed | tf_op | source)
XLA Modules:
  0.0 1665.5 jit_solution(12029237201135259335)
XLA Ops:
  10.0 54.7 %all_gather.34 = bf16[896,1,576]{2,0,1:T(8,128)(2,1)S(1)} all-gather(bf16[56,1,576]{2,0,1:T(8,128)(2,1)} %param.21), channel_id=1, replica_groups=mesh['fsdp'=4,'ctx'=4,'tp'=2] {'fsdp','ctx'}, dimensions={0}, use_global_device_ids=true | all-gather | bytes 1096704 | tf_op jit(solution)/shard_map/all_gather | solution.py:97
  153.8 79.8 %while.26 = (s32[]{:T(128)}, bf16[2,512,1,7,64]{1,4,3,2,0:T(8,128)(2,1)S(1)}, f32[2,1,7,512,1]{3,2,4,1,0:T(8,128)S(1)}, bf16[2,2048,1,128]{1,3,2,0:T(8,128)(2,1)...) while((s32[]{:T(128)}, ...), condition=%wide.region_4.5_spmd.clone, body=%wide.region_1.4_spmd.sunk.clone | while | flops 1970271232 | bytes 95383656 | solution.py:136
  155.9 11.9 fusion.158
  167.8 12.8 fusion.159
  180.6 13.0 fusion.160
  195.8 11.9 fusion.158
  207.7 12.8 fusion.159
  220.5 13.0 fusion.160
  264.5 81.2 %all-gather.12.cloned.1.call-done = bf16[896,2432]{1,0:T(8,128)(2,1)} async-done(((bf16[56,2432]{1,0:T(8,128)(2,1)}), bf16[896,2432]{1,0:T(8,128)(2,1)}) %all-gather.12.cloned.1.call-update) | async-done | bytes 4358160 | tf_op jit(solution)/shard_map/all_gather | solution.py:149
  345.7 10.6 fusion.83
  356.4 68.0 %all-gather.14.cloned.1.call-done = bf16[896,2432]{1,0:T(8,128)(2,1)} async-done(((bf16[56,2432]{1,0:T(8,128)(2,1)}), bf16[896,2432]{1,0:T(8,128)(2,1)}) %all-gather.14.cloned.1.call-update) | async-done | bytes 4358160 | tf_op jit(solution)/shard_map/all_gather | solution.py:150
  434.8 68.3 %all-gather.16.cloned.1.call-done = bf16[896,2432]{1,0:T(8,128)(2,1)} async-done(((bf16[56,2432]{1,0:T(8,128)(2,1)}), bf16[896,2432]{1,0:T(8,128)(2,1)}) %all-gather.16.cloned.1.call-update) | async-done | bytes 4358160 | tf_op jit(solution)/shard_map/all_gather | solution.py:151
  503.1 16.9 %multiply_convert_fusion = (bf16[1024,2432]{1,0:T(8,128)(2,1)}, bf16[1024,2432]{1,0:T(8,128)(2,1)S(1)}, bf16[1024,2432]{1,0:T(8,128)(2,1)}) fusion(f32[1024,2432]{1,0:T(8,128)} %fusion.83, f32[1024,2432]{1,0:T(8,128)} %fusion.84, bf16[1024,896]{1,0:T(8,128)(2,1)} %bitcast.347, bf16[896,2432]{1,0:T(8,128)(2,1)} %all-gather.16.cloned.1.call-done), kind=kOutput, calls=%fused_computation.67 | convolution fusion | flops 4500094976 | bytes 41058304 | tf_op jit(solution)/shard_map/dot_general | solution.py:189
  548.8 50.4 %all_gather.41 = bf16[896,448]{1,0:T(8,128)(2,1)S(1)} all-gather(bf16[56,448]{1,0:T(8,128)(2,1)S(1)} %copy-done.27), channel_id=1, replica_groups=mesh['fsdp'=4,'ctx'=4,'tp'=2] {'fsdp','ctx'}, dimensions={0}, use_global_device_ids=true | all-gather | bytes 852992 | tf_op jit(solution)/shard_map/all_gather | solution.py:177
  604.7 187.2 %while.27 = (s32[]{:T(128)}, f32[2,512,1,7,64]{1,4,3,2,0:T(8,128)}, bf16[2,2048,1,128]{1,3,2,0:T(8,128)(2,1)}, bf16[2,2048,1,128]{1,3,2,0:T(8,128)(2,1)}, s32[2,...) while((s32[]{:T(128)}, f32[2,512,1,7,64]{1,4,3,2,0:T(8,128)}, ...), condition=%wide.region_12.13_spmd.clone, body=%wide.region_10.12_spmd.sunk.clone | while | flops 4768363520 | bytes 228568192 | solution.py:263
  606.2 11.8 fusion.167
  619.0 21.3 %fusion.169 = (f32[7,512]{1,0:T(8,128)S(1)}, f32[1,7,512,2048]{2,3,1,0:T(8,128)}) fusion(f32[2048,512,7]{1,0,2:T(8,128)} %fusion.167, f32[7,512]{1,0:T(8,128)S(1)} %dynamic-slice_bitcast_fusion.11, bf16[2,512,1,7,64]{1,4,3,2,0:T(8,128)(2,1)S(1)} %get-tuple-element.480, s32[]{:T(128)} %get-tuple-element.463, ...), kind=kOutput, calls=%fused_computation.29.clone.1.clone | convolution fusion | flops 976220672 | bytes 60520452 | tf_op jit(solution)/shard_map/while/body/eval_jaxpr/qhgd,khd->hgqk/dot_general | solution.py:59
  640.3 25.0 %fusion.170 = bf16[7,512,2048]{1,2,0:T(8,128)(2,1)} fusion(f32[1,7,512,2048]{2,3,1,0:T(8,128)} %get-tuple-element.416, f32[2048,512,7]{1,0,2:T(8,128)} %fusion.167, f32[7,512]{1,0:T(8,128)S(1)} %get-tuple-element.417), kind=kLoop, calls=%fused_computation.32.clone.1.clone | loop fusion | flops 22020096 | bytes 73414656 | tf_op jit(solution)/shard_map/reshape.37
  675.0 13.9 fusion.172
  699.5 11.8 fusion.167
  712.3 21.3 %fusion.169 = (f32[7,512]{1,0:T(8,128)S(1)}, f32[1,7,512,2048]{2,3,1,0:T(8,128)}) fusion(f32[2048,512,7]{1,0,2:T(8,128)} %fusion.167, f32[7,512]{1,0:T(8,128)S(1)} %dynamic-slice_bitcast_fusion.11, bf16[2,512,1,7,64]{1,4,3,2,0:T(8,128)(2,1)S(1)} %get-tuple-element.480, s32[]{:T(128)} %get-tuple-element.463, ...), kind=kOutput, calls=%fused_computation.29.clone.1.clone | convolution fusion | flops 976220672 | bytes 60520452 | tf_op jit(solution)/shard_map/while/body/eval_jaxpr/qhgd,khd->hgqk/dot_general | solution.py:59
  733.6 25.0 %fusion.170 = bf16[7,512,2048]{1,2,0:T(8,128)(2,1)} fusion(f32[1,7,512,2048]{2,3,1,0:T(8,128)} %get-tuple-element.416, f32[2048,512,7]{1,0,2:T(8,128)} %fusion.167, f32[7,512]{1,0:T(8,128)S(1)} %get-tuple-element.417), kind=kLoop, calls=%fused_computation.32.clone.1.clone | loop fusion | flops 22020096 | bytes 73414656 | tf_op jit(solution)/shard_map/reshape.37
  768.3 13.9 fusion.172
  794.6 20.9 %reduce-scatter.22.cloned.1.call-done = bf16[2,512,1,128]{1,3,2,0:T(8,128)(2,1)} async-done(((bf16[2,2048,1,128]{1,3,2,0:T(8,128)(2,1)}), bf16[2,512,1,128]{1,3,2,0:T(8,128)(2,1)}) %reduce-scatter.22.cloned.1.call-update) | async-done | bytes 262160 | tf_op jit(solution)/shard_map/reduce_scatter | solution.py:266
  847.6 11.9 convolution_bitcast_fusion.1
  871.6 11.5 fusion.88
  883.1 10.8 fusion.87
  897.7 48.3 %all-reduce.4 = (f32[2,896]{1,0:T(2,128)S(1)}, f32[1,576]{1,0:T(1,128)}) all-reduce(f32[2,896]{1,0:T(2,128)S(1)} %convert_reduce_fusion.1, f32[1,576]{1,0:T(1,128)S(1)} %reshape.576), channel_id=1, replica_groups=mesh['fsdp'=4,'ctx'=4,'tp'=2] {'fsdp','ctx'}, use_global_device_ids=true, to_apply=%region_19.20 | all-reduce | flops 2368 | bytes 18944 | tf_op jit(solution)/shard_map/psum | solution.py:311
  950.2 243.6 %all-reduce.8.cloned.1.call-done = (f32[896,1,576]{2,1,0:T(1,128)}, f32[896,2432]{0,1:T(8,128)}) async-done(((f32[896,1,576]{2,1,0:T(1,128)}, f32[896,2432]{0,1:T(8,128)}), (f32[896,1,576]{2,1,0:T(1,128)}, f32[896,2432]{0,1:T(8,128)})) %all-reduce.8.cloned.1.call-update) | async-done | bytes 10780688
  1198.6 79.3 %reduce-scatter.26.cloned.1.call-done = f32[56,448]{1,0:T(8,128)} async-done(((f32[896,448]{1,0:T(8,128)}), f32[56,448]{1,0:T(8,128)}) %reduce-scatter.26.cloned.1.call-update) | async-done | bytes 100368 | tf_op jit(solution)/shard_map/reduce_scatter | solution.py:285
  1277.9 190.1 %reduce-scatter.30.cloned.1.call-done = f32[56,2432]{1,0:T(8,128)} async-done(((f32[896,2432]{1,0:T(8,128)}), f32[56,2432]{1,0:T(8,128)}) %reduce-scatter.30.cloned.1.call-update) | async-done | bytes 544784
  1468.0 190.7 %reduce-scatter.28.cloned.1.call-done = f32[56,2432]{1,0:T(8,128)} async-done(((f32[896,2432]{1,0:T(8,128)}), f32[56,2432]{1,0:T(8,128)}) %reduce-scatter.28.cloned.1.call-update) | async-done | bytes 544784
  (315 shorter events, 271.9 us)
Async XLA Ops:
  7.2 145.7 %all-gather.8.cloned.1.call-start = ((), (), s32[]{:S(2)}) async-start(), calls=%async_computation.8 | async-start | bytes 1310720 | tf_op jit(solution)/shard_map/all_gather | solution.py:121
  76.7 172.8 %reduce-scatter.16.cloned.1.call-start = ((), (), s32[]{:S(2)}) async-start(), calls=%async_computation.9 | async-start | bytes 2752512 | tf_op jit(solution)/shard_map/reduce_scatter | solution.py:141
  76.8 7.9 collective-permute-start
  76.9 9.0 collective-permute-start.1
  84.7 9.0 collective-permute-start.2
  85.8 9.0 collective-permute-start.3
  93.6 9.0 collective-permute-start.4
  94.9 9.0 collective-permute-start.5
  102.6 8.6 collective-permute-start.6
  103.9 7.9 collective-permute-start.7
  111.2 8.0 collective-permute-start.8
  111.8 8.1 collective-permute-start.9
  119.2 8.1 collective-permute-start.10
  119.8 7.7 collective-permute-start.11
  127.3 7.8 collective-permute-start.12
  127.5 21.4 %collective-permute-start.13 = (bf16[56,448]{1,0:T(8,128)(2,1)S(1)}, bf16[56,448]{1,0:T(8,128)(2,1)}, u32[]{:S(2)}, u32[]{:S(2)}) collective-permute-start(bf16[56,448]{1,0:T(8,128)(2,1)S(1)} %collective-permute-done.11), channel_id=1, source_target_pairs={{0,30},{2,0},{4,2},{6,4},{8,6},{10,8},{12,10},{14,12},{16,14},{18,... | collective-permute-start | bytes 150536 | tf_op jit(solution)/shard_map/ppermute | solution.py:36
  135.0 16.1 collective-permute-start.14
  238.7 25.8 %all-gather.10.cloned.1.call-start = ((), (), s32[]{:S(2)}) async-start(), calls=%async_computation.10 | async-start | bytes 2752512 | tf_op jit(solution)/shard_map/all_gather | solution.py:158
  240.8 306.3 %copy-start.28 = (f32[896]{0:T(1024)}, f32[896]{0:T(1024)S(1)}, u32[]{:S(2)}) copy-start(f32[896]{0:T(1024)S(1)} %convert_element_type.195) | copy-start | bytes 10756
  253.0 92.7 %all-gather.12.cloned.1.call-start = ((), (), s32[]{:S(2)}) async-start(), calls=%async_computation.11 | async-start | bytes 4630528 | tf_op jit(solution)/shard_map/all_gather | solution.py:149
  253.6 170.8 %all-gather.14.cloned.1.call-start = ((), (), s32[]{:S(2)}) async-start(), calls=%async_computation.12 | async-start | bytes 4630528 | tf_op jit(solution)/shard_map/all_gather | solution.py:150
  254.2 248.9 %all-gather.16.cloned.1.call-start = ((), (), s32[]{:S(2)}) async-start(), calls=%async_computation.13 | async-start | bytes 4630528 | tf_op jit(solution)/shard_map/all_gather | solution.py:151
  254.8 289.7 %reduce-scatter.20.cloned.1.call-start = ((), (), s32[]{:S(2)}) async-start(), calls=%async_computation.15 | async-start | bytes 2752512 | tf_op jit(solution)/shard_map/reduce_scatter | solution.py:215
  536.3 62.8 %all-gather.18.cloned.1.call-start = ((), (), s32[]{:S(2)}) async-start(), calls=%async_computation.16 | async-start | bytes 2752512 | tf_op jit(solution)/shard_map/all_gather | solution.py:227
  548.7 266.9 %reduce-scatter.22.cloned.1.call-start = ((), (), s32[]{:S(2)}) async-start(), calls=%async_computation.17 | async-start | bytes 1310720 | tf_op jit(solution)/shard_map/reduce_scatter | solution.py:266
  792.0 40.7 %reduce-scatter.24.cloned.1.call-start = ((), (), s32[]{:S(2)}) async-start(), calls=%async_computation.18 | async-start | bytes 2752512 | tf_op jit(solution)/shard_map/reduce_scatter | solution.py:287
  822.8 21.0 %reduce-scatter.18.cloned.1.call-start = ((), (), s32[]{:S(2)}) async-start(), calls=%async_computation.14 | async-start | bytes 2752512 | tf_op jit(solution)/shard_map/reduce_scatter | solution.py:168
  832.6 114.1 %all-gather.20.cloned.1.call-start = ((), (), s32[]{:S(2)}) async-start(), calls=%async_computation.19 | async-start | bytes 2752512 | tf_op jit(solution)/shard_map/all_gather | solution.py:302
  847.6 346.2 %all-reduce.8.cloned.1.call-start = ((), (), s32[]{:S(2)}) async-start(), calls=%async_computation.23 | async-start | bytes 22020096
  866.2 411.8 %reduce-scatter.26.cloned.1.call-start = ((), (), s32[]{:S(2)}) async-start(), calls=%async_computation.20 | async-start | bytes 1949696 | tf_op jit(solution)/shard_map/reduce_scatter | solution.py:285
  871.3 596.8 %reduce-scatter.30.cloned.1.call-start = ((), (), s32[]{:S(2)}) async-start(), calls=%async_computation.22 | async-start | bytes 9261056
  883.1 775.7 %reduce-scatter.28.cloned.1.call-start = ((), (), s32[]{:S(2)}) async-start(), calls=%async_computation.21 | async-start | bytes 9261056
  (52 other events, 1201.5 us)
Sparse Core Ops, SparseCore 0:
  76.9 31.2 all-gather.7
  238.8 10.6 reduce-scatter.15
  253.1 11.3 all-gather.9
  267.4 78.2 all-gather.11
  348.6 75.7 all-gather.13
  427.3 75.7 all-gather.15
  536.4 7.9 reduce-scatter.19
  548.8 11.3 all-gather.17
  792.1 23.3 reduce-scatter.21
  822.9 8.0 reduce-scatter.23
  833.2 10.4 reduce-scatter.17
  847.7 11.3 all-gather.19
  866.6 327.0 all-reduce.7
  1196.6 81.2 reduce-scatter.25
  1280.7 187.3 reduce-scatter.29
  1470.8 187.9 reduce-scatter.27
